TPU v7x, 32 devices: a whole 2x2x4 slice. The times are simulated.
32 devices in a mesh: kv: 4 (over y, x), seq: 8 (over z, core).
Axes of the slice: x: 2, y: 2, z: 4, core: 2. Of those that a mesh axis runs over, the one named last changes fastest.
Arguments:
- queries: bfloat16 [1024, 12288], P('seq', 'kv'), may hold values from -400 to 400
- cache_keys: bfloat16 [8192, 768], P('seq', 'kv'), may hold values from -6 to 6
- cache_values: bfloat16 [8192, 512], P('seq', 'kv'), may hold values from -6 to 6
- incoming_keys: bfloat16 [1024, 768], P('seq', 'kv'), may hold values from -6 to 6
- new_values: bfloat16 [1024, 512], P('seq', 'kv'), may hold values from -6 to 6
- comp_key_weight: bfloat16 [6144, 192], P('kv'), may hold values from -0.078125 to 0.078125
- comp_value_weight: bfloat16 [4096, 128], P('kv'), may hold values from -0.09375 to 0.09375
- select_blocks: int32 [32, 4, 16], P('seq', 'kv'), may hold values from 0 to 127, as said below
- gate_weight: bfloat16 [64, 192, 3], P('kv'), may hold values from -0.4375 to 0.4375
Outputs:
- attended: bfloat16 [1024, 8192], P('seq', 'kv')
Inputs may be any that keep to these rules, and one draw needn't show every extreme that they name: `select_blocks`: each row names 16 different blocks. For each KV group, the rows of one device of seq (4 tiles) name blocks of any one cache shard (the 16 blocks of one index of seq) at most 16 times in all, and in every draw the rows of every device name one shard's blocks exactly 16 times.
All inputs are finite; a program needn't handle non-finite values.
Results may differ from a plain program's by a relative error of at most 0.012.
Values may be sent and summed in bfloat16 or wider, within the bound.
A program may use at most 128 MiB of HBM per device.

v0:
```python
import jax
import jax.numpy as jnp
from jax import lax
from jax.sharding import PartitionSpec as P

CMP_STRIDE = 16
SEL_BLOCK = 64
WINDOW = 512
MASKED = -1e30


def passed_along(block, axis, distance):
    devices = range(lax.axis_size(axis))
    route = [((i - distance) % len(devices), i) for i in devices]
    return lax.ppermute(block, axis, route)


def from_behind(x, axis, by):
    peers = lax.axis_size(axis)
    pairs = [(i, i + by) for i in range(peers) if 0 <= i + by < peers]
    return lax.ppermute(x, axis, pairs)


def pack_rows(keys, values):
    return jnp.concatenate([keys.reshape(-1), values.reshape(-1)])


def unpack_rows(flat, count, key_width, value_width):
    keys = flat[: count * key_width].reshape(count, key_width)
    values = flat[count * key_width : count * (key_width + value_width)].reshape(count, value_width)
    return (keys, values)


def finish_rows(scores, values):
    top = jnp.max(scores, axis=-1, keepdims=True)
    weights = jnp.exp(scores - top)
    total = jnp.sum(weights, axis=-1, keepdims=True)
    mixed = jnp.matmul(weights.astype(jnp.bfloat16), values, preferred_element_type=jnp.float32)
    return mixed / total


def shards(
    queries,
    cache_keys,
    cache_values,
    incoming_keys,
    new_values,
    comp_key_weight,
    comp_value_weight,
    select_blocks,
    gate_weight,
):
    heads, key_width, _ = gate_weight.shape
    value_width = cache_values.shape[1]
    query_count = queries.shape[0]
    cache_count = cache_keys.shape[0]
    ranks = lax.axis_size("seq")
    place = lax.axis_index("seq")
    scale = key_width ** (-0.5)
    rows = queries.reshape(query_count * heads, key_width)
    row_total = rows.shape[0]
    stretch_pos = place * query_count + jnp.arange(query_count, dtype=jnp.int32)
    lookback_length = -(-WINDOW // query_count)
    weight_keys, weight_values = (
        lax.all_gather(comp_key_weight, "kv", axis=0, tiled=True),
        lax.all_gather(comp_value_weight, "kv", axis=0, tiled=True),
    )
    tail_pack = pack_rows(cache_keys[cache_count - WINDOW :], cache_values[cache_count - WINDOW :])
    moved_tail = passed_along(tail_pack, "seq", 1)
    before_keys, before_values = unpack_rows(moved_tail, WINDOW, key_width, value_width)
    edge_keys = before_keys[WINDOW - CMP_STRIDE :]
    edge_values = before_values[WINDOW - CMP_STRIDE :]
    held_tail = jnp.where(place == 0, moved_tail, jnp.zeros_like(moved_tail))
    tail_size = held_tail.shape[0]
    tail_flat = held_tail
    near_keys = []
    near_values = []
    nearby_positions = []
    near_valid = []
    own = pack_rows(incoming_keys, new_values)
    own_size = own.shape[0]
    for back in range(lookback_length, 0, -1):
        moved = from_behind(jnp.concatenate([own, held_tail]), "seq", back)
        got_keys, got_values = unpack_rows(moved, query_count, key_width, value_width)
        tail_flat = jnp.where(place == back, moved[own_size : own_size + tail_size], tail_flat)
        near_keys.append(got_keys)
        near_values.append(got_values)
        nearby_positions.append(
            (place - back) * query_count + jnp.arange(query_count, dtype=jnp.int32)
        )
        near_valid.append(jnp.broadcast_to(place >= back, (query_count,)))
    tail_keys, tail_values = unpack_rows(tail_flat, WINDOW, key_width, value_width)
    near_keys.append(tail_keys)
    near_values.append(tail_values)
    nearby_positions.append(jnp.arange(WINDOW, dtype=jnp.int32) - WINDOW)
    near_valid.append(jnp.ones((WINDOW,), dtype=bool))
    near_keys.append(incoming_keys)
    near_values.append(new_values)
    nearby_positions.append(stretch_pos)
    near_valid.append(jnp.ones((query_count,), dtype=bool))
    half_keys = CMP_STRIDE * key_width
    half_values = CMP_STRIDE * value_width
    lead_keys = jnp.concatenate([edge_keys, cache_keys[: cache_count - CMP_STRIDE]]).reshape(
        -1, half_keys
    )
    lead_values = jnp.concatenate([edge_values, cache_values[: cache_count - CMP_STRIDE]]).reshape(
        -1, half_values
    )
    comp_keys = (
        jnp.dot(lead_keys, weight_keys[:half_keys], preferred_element_type=jnp.float32)
        + jnp.dot(
            cache_keys.reshape(-1, half_keys),
            weight_keys[half_keys:],
            preferred_element_type=jnp.float32,
        )
    ).astype(jnp.bfloat16)
    comp_values = (
        jnp.dot(lead_values, weight_values[:half_values], preferred_element_type=jnp.float32)
        + jnp.dot(
            cache_values.reshape(-1, half_values),
            weight_values[half_values:],
            preferred_element_type=jnp.float32,
        )
    ).astype(jnp.bfloat16)
    start = jnp.int32(0)
    top = jnp.full((row_total,), MASKED, jnp.float32)
    total = jnp.zeros((row_total,), jnp.float32)
    summed = jnp.zeros((row_total, value_width), jnp.float32)
    keys = lax.all_gather(comp_keys, "seq", axis=0, tiled=True)
    values = lax.all_gather(comp_values, "seq", axis=0, tiled=True)
    length = keys.shape[0]
    block = length
    for size in (1024, 512, 256, 128):
        if length % size == 0:
            block = size
            break
    for index in range(length // block):
        key_block = keys[index * block : (index + 1) * block]
        value_block = values[index * block : (index + 1) * block]
        scores = (
            jnp.einsum("rd,kd->rk", rows, key_block, preferred_element_type=jnp.float32) * scale
        )
        key_at = start + index * block + jnp.arange(block, dtype=jnp.int32)
        scores = jnp.where(key_at[None, :] > 0, scores, MASKED)
        newtop = jnp.maximum(top, jnp.max(scores, axis=1))
        factor = jnp.exp(top - newtop)
        weights = jnp.exp(scores - newtop[:, None])
        total = total * factor + jnp.sum(weights, axis=1)
        summed = summed * factor[:, None] + jnp.dot(
            weights.astype(jnp.bfloat16), value_block, preferred_element_type=jnp.float32
        )
        top = newtop
    top, total, summed = (top, total, summed)
    compressed_out = summed / total[:, None]
    chosen = select_blocks.reshape(-1)
    shard_blocks = cache_count // SEL_BLOCK
    capacity = max(2, 2 * chosen.shape[0] // ranks)
    owner = chosen // shard_blocks
    local = chosen - owner * shard_blocks
    onehot = (owner[:, None] == jnp.arange(ranks, dtype=jnp.int32)[None, :]).astype(jnp.int32)
    position = jnp.sum((jnp.cumsum(onehot, axis=0) - 1) * onehot, axis=1)
    request = jnp.full((ranks, capacity), -1, jnp.int32).at[owner, position].set(local)
    key_blocks = cache_keys.reshape(shard_blocks, SEL_BLOCK, key_width)
    value_block_list = cache_values.reshape(shard_blocks, SEL_BLOCK, value_width)
    safe = jnp.clip(
        lax.all_to_all(request, "seq", split_axis=0, concat_axis=0, tiled=True), 0, shard_blocks - 1
    )
    got_keys = lax.all_to_all(key_blocks[safe], "seq", split_axis=0, concat_axis=0, tiled=True)
    got_values = lax.all_to_all(
        value_block_list[safe], "seq", split_axis=0, concat_axis=0, tiled=True
    )
    where_at = owner * capacity + position
    tile_count = select_blocks.shape[0]
    gathered_keys = got_keys.reshape(ranks * capacity, SEL_BLOCK, key_width)[where_at]
    picked_values = got_values.reshape(ranks * capacity, SEL_BLOCK, value_width)[where_at]
    gathered_keys, picked_values = (
        gathered_keys.reshape(tile_count, -1, key_width),
        picked_values.reshape(tile_count, -1, value_width),
    )
    tile_count = gathered_keys.shape[0]
    tile_row_count = rows.reshape(tile_count, -1, key_width)
    tile_scores = (
        jnp.einsum(
            "izu,ixu->izx", tile_row_count, gathered_keys, preferred_element_type=jnp.float32
        )
        * scale
    )
    selected_out = finish_rows(tile_scores, picked_values).reshape(row_total, value_width)
    context_keys = jnp.concatenate(near_keys)
    context_values = jnp.concatenate(near_values)
    context_positions = jnp.concatenate(nearby_positions)
    context_valid = jnp.concatenate(near_valid)
    sliding_scores = (
        jnp.einsum("rd,kd->rk", rows, context_keys, preferred_element_type=jnp.float32) * scale
    )
    allowed = (
        context_valid[None, :]
        & (context_positions[None, :] <= stretch_pos[:, None])
        & (context_positions[None, :] > stretch_pos[:, None] - WINDOW)
    )
    sliding_scores = jnp.where(
        allowed[:, None, :], sliding_scores.reshape(query_count, heads, -1), MASKED
    )
    window_out = finish_rows(sliding_scores.reshape(row_total, -1), context_values)
    logits = jnp.einsum(
        "thd,hdb->thb",
        queries.reshape(query_count, heads, key_width),
        gate_weight,
        preferred_element_type=jnp.float32,
    )
    gates = jax.nn.sigmoid(logits)
    mixed = (
        gates[:, :, 0:1] * compressed_out.reshape(query_count, heads, value_width)
        + gates[:, :, 1:2] * selected_out.reshape(query_count, heads, value_width)
        + gates[:, :, 2:3] * window_out.reshape(query_count, heads, value_width)
    )
    return mixed.astype(jnp.bfloat16).reshape(query_count, heads * value_width)


def solution(mesh):
    placed = (
        P("seq", "kv"),
        P("seq", "kv"),
        P("seq", "kv"),
        P("seq", "kv"),
        P("seq", "kv"),
        P("kv", None),
        P("kv", None),
        P("seq", "kv", None),
        P("kv", None, None),
    )
    return jax.shard_map(
        shards, mesh=mesh, in_specs=placed, out_specs=P("seq", "kv"), check_vma=False
    )
```

profile of v0, /device:TPU:0, one launch (start us, length us, event | category | flops | bytes accessed | tf_op | source)
XLA Modules:
  0.0 310.4 jit_solution(10423262976556319975)
XLA Ops:
  7.3 0.9 slice.154
  8.7 0.9 slice_bitcast_fusion.1
  9.6 0.7 pad_maximum_fusion.2
  10.8 0.8 reshape.400
  12.3 1.3 reduce.7
  14.6 10.2 %scatter_fusion = s32[8,16]{1,0:T(8,128)} fusion(s32[8,16]{1,0:T(8,128)} %broadcast_in_dim.83, s32[64]{0:T(128)S(1)} %fusion.59, s32[64]{0:T(128)S(1)} %get-tuple-element.7), kind=kCustom, calls=%fused_computation.4 | custom fusion | bytes 1280 | tf_op jit(solution)/shard_map/scatter | solution.py:162
  24.7 6.3 %all-to-all-start = ((s32[8,1,16]{2,1,0:T(1,128)}), s32[8,1,16]{2,1,0:T(1,128)}, u32[]{:S(2)}, u32[]{:S(2)}) async-start(s32[8,1,16]{2,1,0:T(1,128)} %bitcast.10), calls=%async_computation | async-start | bytes 8192 | tf_op jit(solution)/shard_map/all_to_all | solution.py:166
  32.0 2.1 reshape.394
  34.2 2.1 reshape_reshape.6
  40.4 0.7 slice.163
  41.2 0.8 reshape.396
  42.1 0.7 reshape.406
  43.5 2.5 copy.51
  46.0 1.3 reshape.393
  47.3 1.4 copy.36
  49.5 0.7 copy.48
  50.9 2.8 gather_fusion
  53.7 2.2 gather_fusion.2
  55.9 5.1 %all-to-all-start.2 = ((bf16[8,16,64,128]{3,2,1,0:T(8,128)(2,1)}), bf16[8,16,64,128]{3,2,1,0:T(8,128)(2,1)}, u32[]{:S(2)}, u32[]{:S(2)}) async-start(bf16[8,16,64,128]{3,2,1,0:T(8,128)(2,1)} %bitcast.113), calls=%async_computation.2 | async-start | bytes 4194304 | tf_op jit(solution)/shard_map/all_to_all | solution.py:169
  61.0 1.0 broadcast_select_fusion
  62.0 0.8 pad_maximum_fusion
  62.8 4.6 %collective-permute-start.1 = (bf16[204800]{0:T(1024)(128)(2,1)}, bf16[204800]{0:T(1024)(128)(2,1)}, u32[]{:S(2)}, u32[]{:S(2)}) collective-permute-start(bf16[204800]{0:T(1024)(128)(2,1)} %pad_maximum_fusion), channel_id=1, source_target_pairs={{0,4},{1,5},{2,6},{3,7},{8,12},{9,13},{10,14},{11,15},{16,20},{17,... | collective-permute-start | bytes 1228808 | tf_op jit(solution)/shard_map/ppermute | solution.py:21
  67.4 3.6 %collective-permute-start.2 = (bf16[204800]{0:T(1024)(128)(2,1)}, bf16[204800]{0:T(1024)(128)(2,1)}, u32[]{:S(2)}, u32[]{:S(2)}) collective-permute-start(bf16[204800]{0:T(1024)(128)(2,1)} %pad_maximum_fusion), channel_id=1, source_target_pairs={{0,3},{1,4},{2,5},{3,6},{4,7},{8,11},{9,12},{10,13},{11,14},{12,15... | collective-permute-start | bytes 1228808 | tf_op jit(solution)/shard_map/ppermute | solution.py:21
  71.0 2.6 collective-permute-start.3
  73.6 2.1 collective-permute-start.4
  77.3 1.0 pad_maximum_fusion.1
  78.3 1.2 copy.39
  79.5 1.3 reshape.392
  80.8 1.0 pad_maximum_fusion.3
  81.9 23.0 %collective-permute-done.1 = bf16[204800]{0:T(1024)(128)(2,1)} collective-permute-done((bf16[204800]{0:T(1024)(128)(2,1)}, bf16[204800]{0:T(1024)(128)(2,1)}, u32[]{:S(2)}, u32[]{:S(2)}) %collective-permute-start.1) | collective-permute-done | bytes 409632 | tf_op jit(solution)/shard_map/ppermute | solution.py:21
  104.9 1.4 fusion.54
  106.3 7.4 %collective-permute-done.2 = bf16[204800]{0:T(1024)(128)(2,1)} collective-permute-done((bf16[204800]{0:T(1024)(128)(2,1)}, bf16[204800]{0:T(1024)(128)(2,1)}, u32[]{:S(2)}, u32[]{:S(2)}) %collective-permute-start.2) | collective-permute-done | bytes 409632 | tf_op jit(solution)/shard_map/ppermute | solution.py:21
  113.7 1.4 fusion.53
  115.0 7.4 %collective-permute-done.3 = bf16[204800]{0:T(1024)(128)(2,1)} collective-permute-done((bf16[204800]{0:T(1024)(128)(2,1)}, bf16[204800]{0:T(1024)(128)(2,1)}, u32[]{:S(2)}, u32[]{:S(2)}) %collective-permute-start.3) | collective-permute-done | bytes 409632 | tf_op jit(solution)/shard_map/ppermute | solution.py:21
  122.5 1.4 fusion.49
  123.9 1.4 fusion.52
  125.5 0.8 slice.206
  126.4 0.8 slice.207
  127.3 0.8 slice.208
  128.2 0.8 slice.209
  129.1 1.4 fusion.51
  130.5 33.3 %all-to-all-start.1 = ((bf16[8,16,64,192]{3,2,1,0:T(8,128)(2,1)}), bf16[8,16,64,192]{3,2,1,0:T(8,128)(2,1)}, u32[]{:S(2)}, u32[]{:S(2)}) async-start(bf16[8,16,64,192]{3,2,1,0:T(8,128)(2,1)} %bitcast.110), calls=%async_computation.1 | async-start | bytes 8388608 | tf_op jit(solution)/shard_map/all_to_all | solution.py:168
  164.4 1.4 constant_dynamic-update-slice_fusion.7
  165.8 3.2 %fusion.65 = (f32[2048]{0:T(1024)S(1)}, f32[2048,1152]{0,1:T(8,128)S(1)}) fusion(pred[2048,1152]{0,1:T(32,128)(4,1)S(1)} %copy.51, bf16[1152,192]{1,0:T(8,128)(2,1)S(1)} %constant_dynamic-update-slice_fusion.1, bf16[2048,192]{1,0:T(8,128)(2,1)} %reshape.394), kind=kOutput, calls=%fused_computation.126 | convolution fusion | flops 913045504 | bytes 13033472 | tf_op jit(solution)/shard_map/rd,kd->rk/dot_general | solution.py:194
  169.0 1.4 fusion.1
  170.4 1.8 fusion.16
  172.3 1.1 reshape.413
  173.4 1.3 fusion.45
  174.7 1.3 fusion.37
  176.0 88.1 %all_gather.15 = bf16[512,128]{1,0:T(8,128)(2,1)S(1)} all-gather(bf16[64,128]{1,0:T(8,128)(2,1)S(1)} %fusion.37), channel_id=1, replica_groups=mesh['kv'=4,'seq'=8] {'seq'}, dimensions={0}, use_global_device_ids=true | all-gather | bytes 147456 | tf_op jit(solution)/shard_map/all_gather | solution.py:130
  264.1 1.8 fusion.23
  265.9 1.9 fusion.30
  267.8 14.4 %all_gather.13 = bf16[512,192]{1,0:T(8,128)(2,1)S(1)} all-gather(bf16[64,192]{1,0:T(8,128)(2,1)S(1)} %fusion.30), channel_id=1, replica_groups=mesh['kv'=4,'seq'=8] {'seq'}, dimensions={0}, use_global_device_ids=true | all-gather | bytes 221184 | tf_op jit(solution)/shard_map/all_gather | solution.py:129
  282.2 0.9 fusion.12
  283.1 0.9 fusion.13
  284.0 1.5 fusion.15
  285.6 1.1 reshape.397
  286.7 3.4 %gather_fusion.3 = bf16[64,64,128]{2,1,0:T(8,128)(2,1)} fusion(bf16[128,64,128]{2,1,0:T(8,128)(2,1)} %bitcast.20, s32[1024]{0:T(1024)} %pad_clamp_fusion), kind=kCustom, calls=%fused_computation.3 | custom fusion | bytes 2097408 | tf_op jit(solution)/shard_map/gather | solution.py:175
  290.1 3.0 gather_fusion.1
  293.1 1.3 bitcast_reduce_fusion
  294.4 1.4 fusion.3
  295.8 3.2 %fusion.41 = f32[4,512,128]{2,1,0:T(8,128)} fusion(bf16[4,1024,128]{2,1,0:T(8,128)(2,1)S(1)} %bitcast.119, f32[4,1024,512]{2,1,0:T(8,128)S(1)} %get-tuple-element.17, f32[4,512]{1,0:T(4,128)S(1)} %get-tuple-element.16, f32[4,512]{1,0:T(4,128)S(1)} %fusion.3), kind=kOutput, calls=%fused_computation.50 | convolution fusion | flops 543424512 | bytes 10502144 | tf_op jit(solution)/shard_map/dot_general | solution.py:38
  299.0 1.5 reshape_reshape.7
  301.6 1.9 fusion.39
  (121 shorter events, 14.5 us)
Async XLA Ops:
  6.5 25.3 %copy-start.6 = (bf16[1024,192]{0,1:T(8,128)(2,1)S(1)}, bf16[1024,192]{0,1:T(8,128)(2,1)}, u32[]{:S(2)}) copy-start(bf16[1024,192]{0,1:T(8,128)(2,1)} %param.10) | copy-start | bytes 1179652
  6.5 25.5 %copy-start.1 = (bf16[128,3072]{1,0:T(8,128)(2,1)S(1)}, bf16[128,3072]{1,0:T(8,128)(2,1)}, u32[]{:S(2)}) copy-start(bf16[128,3072]{1,0:T(8,128)(2,1)} %param.9) | copy-start | bytes 2359300
  6.5 166.9 %all-gather.5.cloned.1.call-start = ((), (), s32[]{:S(2)}) async-start(), calls=%async_computation.4 | async-start | bytes 1310720 | tf_op jit(solution)/shard_map/all_gather | solution.py:66
  10.3 28.9 %copy-start.18 = (bf16[16,192,3]{1,0,2:T(8,128)(2,1)S(1)}, bf16[16,192,3]{1,0,2:T(8,128)(2,1)}, u32[]{:S(2)}) copy-start(bf16[16,192,3]{1,0,2:T(8,128)(2,1)} %param.17) | copy-start | bytes 55300
  10.3 50.6 %collective-permute-start = (bf16[163840]{0:T(1024)(128)(2,1)}, bf16[163840]{0:T(1024)(128)(2,1)}, u32[]{:S(2)}, u32[]{:S(2)}) collective-permute-start(bf16[163840]{0:T(1024)(128)(2,1)} %pad_maximum_fusion.2), channel_id=1, source_target_pairs={{7,0},{0,1},{1,2},{2,3},{3,4},{4,5},{5,6},{6,7},{15,8},{8,9},{9,10... | collective-permute-start | bytes 983048 | tf_op jit(solution)/shard_map/ppermute | solution.py:15
  24.7 15.7 %copy-start = (bf16[1024,128]{1,0:T(8,128)(2,1)S(1)}, bf16[1024,128]{1,0:T(8,128)(2,1)}, u32[]{:S(2)}) copy-start(bf16[1024,128]{1,0:T(8,128)(2,1)} %param.11) | copy-start | bytes 786436
  24.7 25.5 %all-to-all-start = ((s32[8,1,16]{2,1,0:T(1,128)}), s32[8,1,16]{2,1,0:T(1,128)}, u32[]{:S(2)}, u32[]{:S(2)}) async-start(s32[8,1,16]{2,1,0:T(1,128)} %bitcast.10), calls=%async_computation | async-start | bytes 8192 | tf_op jit(solution)/shard_map/all_to_all | solution.py:166
  31.0 233.1 %all-gather.3.cloned.1.call-start = ((), (), s32[]{:S(2)}) async-start(), calls=%async_computation.3 | async-start | bytes 2949120 | tf_op jit(solution)/shard_map/all_gather | solution.py:65
  31.7 10.3 %copy-start.17 = (bf16[128,192]{0,1:T(8,128)(2,1)S(1)}, bf16[128,192]{0,1:T(8,128)(2,1)}, u32[]{:S(2)}) copy-start(bf16[128,192]{0,1:T(8,128)(2,1)} %param.12) | copy-start | bytes 147460
  42.1 1.4 copy-start.9
  53.7 8.3 %copy-start.15 = (bf16[24576]{0:T(1024)(128)(2,1)S(1)}, bf16[24576]{0:T(1024)(128)(2,1)}, u32[]{:S(2)}) copy-start(bf16[24576]{0:T(1024)(128)(2,1)} %reshape.406) | copy-start | bytes 147460
  53.7 8.3 %copy-start.16 = (bf16[128,128]{1,0:T(8,128)(2,1)S(1)}, bf16[128,128]{1,0:T(8,128)(2,1)}, u32[]{:S(2)}) copy-start(bf16[128,128]{1,0:T(8,128)(2,1)} %param.13) | copy-start | bytes 98308
  55.9 74.6 %all-to-all-start.2 = ((bf16[8,16,64,128]{3,2,1,0:T(8,128)(2,1)}), bf16[8,16,64,128]{3,2,1,0:T(8,128)(2,1)}, u32[]{:S(2)}, u32[]{:S(2)}) async-start(bf16[8,16,64,128]{3,2,1,0:T(8,128)(2,1)} %bitcast.113), calls=%async_computation.2 | async-start | bytes 4194304 | tf_op jit(solution)/shard_map/all_to_all | solution.py:169
  62.8 42.1 %collective-permute-start.1 = (bf16[204800]{0:T(1024)(128)(2,1)}, bf16[204800]{0:T(1024)(128)(2,1)}, u32[]{:S(2)}, u32[]{:S(2)}) collective-permute-start(bf16[204800]{0:T(1024)(128)(2,1)} %pad_maximum_fusion), channel_id=1, source_target_pairs={{0,4},{1,5},{2,6},{3,7},{8,12},{9,13},{10,14},{11,15},{16,20},{17,... | collective-permute-start | bytes 1228808 | tf_op jit(solution)/shard_map/ppermute | solution.py:21
  67.4 46.3 %collective-permute-start.2 = (bf16[204800]{0:T(1024)(128)(2,1)}, bf16[204800]{0:T(1024)(128)(2,1)}, u32[]{:S(2)}, u32[]{:S(2)}) collective-permute-start(bf16[204800]{0:T(1024)(128)(2,1)} %pad_maximum_fusion), channel_id=1, source_target_pairs={{0,3},{1,4},{2,5},{3,6},{4,7},{8,11},{9,12},{10,13},{11,14},{12,15... | collective-permute-start | bytes 1228808 | tf_op jit(solution)/shard_map/ppermute | solution.py:21
  71.0 51.5 %collective-permute-start.3 = (bf16[204800]{0:T(1024)(128)(2,1)}, bf16[204800]{0:T(1024)(128)(2,1)}, u32[]{:S(2)}, u32[]{:S(2)}) collective-permute-start(bf16[204800]{0:T(1024)(128)(2,1)} %pad_maximum_fusion), channel_id=1, source_target_pairs={{0,2},{1,3},{2,4},{3,5},{4,6},{5,7},{8,10},{9,11},{10,12},{11,13},... | collective-permute-start | bytes 1228808 | tf_op jit(solution)/shard_map/ppermute | solution.py:21
  73.6 48.9 %collective-permute-start.4 = (bf16[204800]{0:T(1024)(128)(2,1)}, bf16[204800]{0:T(1024)(128)(2,1)}, u32[]{:S(2)}, u32[]{:S(2)}) collective-permute-start(bf16[204800]{0:T(1024)(128)(2,1)} %pad_maximum_fusion), channel_id=1, source_target_pairs={{0,1},{1,2},{2,3},{3,4},{4,5},{5,6},{6,7},{8,9},{9,10},{10,11},{11... | collective-permute-start | bytes 1228808 | tf_op jit(solution)/shard_map/ppermute | solution.py:21
  130.5 35.4 %copy-start.10 = (bf16[128,192]{1,0:T(8,128)(2,1)S(1)}, bf16[128,192]{1,0:T(8,128)(2,1)}, u32[]{:S(2)}) copy-start(bf16[128,192]{1,0:T(8,128)(2,1)} %copy-done.9) | copy-start | bytes 147460
  130.5 159.6 %all-to-all-start.1 = ((bf16[8,16,64,192]{3,2,1,0:T(8,128)(2,1)}), bf16[8,16,64,192]{3,2,1,0:T(8,128)(2,1)}, u32[]{:S(2)}, u32[]{:S(2)}) async-start(bf16[8,16,64,192]{3,2,1,0:T(8,128)(2,1)} %bitcast.110), calls=%async_computation.1 | async-start | bytes 8388608 | tf_op jit(solution)/shard_map/all_to_all | solution.py:168
  169.0 1.4 copy-start.19
  170.4 4.3 %copy-start.8 = (bf16[64,2048]{1,0:T(8,128)(2,1)S(1)}, bf16[64,2048]{1,0:T(8,128)(2,1)}, u32[]{:S(2)}) copy-start(bf16[64,2048]{1,0:T(8,128)(2,1)} %reshape.396) | copy-start | bytes 786436
  170.4 93.7 %copy-start.11 = (bf16[64,3072]{1,0:T(8,128)(2,1)S(1)}, bf16[64,3072]{1,0:T(8,128)(2,1)}, u32[]{:S(2)}) copy-start(bf16[64,3072]{1,0:T(8,128)(2,1)} %reshape.393) | copy-start | bytes 1179652
  172.2 109.9 %copy-start.3 = (bf16[2048,192]{1,0:T(8,128)(2,1)S(1)}, bf16[2048,192]{1,0:T(8,128)(2,1)}, u32[]{:S(2)}) copy-start(bf16[2048,192]{1,0:T(8,128)(2,1)} %reshape.394) | copy-start | bytes 2359300
  172.3 109.9 %copy-start.20 = (pred[512]{0:T(512)(128)(4,1)S(1)}, pred[512]{0:T(512)(128)(4,1)}, u32[]{:S(2)}) copy-start(pred[512]{0:T(512)(128)(4,1)} %iota_compare_fusion.1) | copy-start | bytes 1540
  285.5 7.6 %copy-start.2 = (bf16[4,512,192]{2,1,0:T(8,128)(2,1)S(1)}, bf16[4,512,192]{2,1,0:T(8,128)(2,1)}, u32[]{:S(2)}) copy-start(bf16[4,512,192]{2,1,0:T(8,128)(2,1)} %reshape_reshape.6) | copy-start | bytes 2359300
  294.4 1.4 copy-start.7
  295.8 4.7 %copy-start.12 = (f32[128,16]{1,0:T(8,128)S(1)}, f32[128,16]{1,0:T(8,128)}, u32[]{:S(2)}) copy-start(f32[128,16]{1,0:T(8,128)} %copy.36) | copy-start | bytes 24580
  295.8 5.1 %copy-start.13 = (f32[128,16]{1,0:T(8,128)S(1)}, f32[128,16]{1,0:T(8,128)}, u32[]{:S(2)}) copy-start(f32[128,16]{1,0:T(8,128)} %copy.41) | copy-start | bytes 24580
  299.0 2.2 copy-start.14
  299.0 2.6 copy-start.4
  299.0 2.6 copy-start.5
Sparse Core Ops, SparseCore 0:
  9.2 29.2 all-gather.4
  40.3 37.2 all-gather.2
where the time goes:
time: 312 us; the launch traced here: 310 us
  blocking collectives  103 us (33%)
  local copies, waits for them, and re-layouts  62.8 us (20%)
  starting transfers between devices  58.1 us (19%)
  waiting for transfers between devices  39.3 us (13%)
  matrix products  18.3 us (6%)
  other arithmetic  15.4 us (5%)
  between operations  14 us (4%)
    all_gather x1, blocking collectives, shards(): values = lax.all_gather(comp_values, 'seq', axis=0, tiled=True)  88.1 us
    ppermute x4, waiting for transfers between devices, from_behind(): return lax.ppermute(x, axis, pairs)  37.8 us
    all_to_all x1, starting transfers between devices, shards(): lax.all_to_all(key_blocks[safe], 'seq', split_axis=0, concat_axis=0, tile...  33.3 us
    all_gather x1, blocking collectives, shards(): keys = lax.all_gather(comp_keys, 'seq', axis=0, tiled=True)  14.4 us
    ppermute x4, starting transfers between devices, from_behind(): return lax.ppermute(x, axis, pairs)  12.9 us
    scatter x1, local copies, waits for them, and re-layouts, shards(): jnp.full((ranks, capacity), -1, jnp.int32).at[owner, position].set(local)  10.2 us
    unnamed x61, local copies, waits for them, and re-layouts  8.66 us
    all_to_all x1, starting transfers between devices, shards(): lax.all_to_all(request, 'seq', split_axis=0, concat_axis=0, tiled=True)  6.28 us
  transfers between devices with their start and end apart: 10, of which 3 were waited for; matrix products, arithmetic and copies ran while one was open for 27% of the time, Pallas kernels for 0%

commit v1 on v0

--- a/solution.py
+++ b/solution.py
@@ -127,7 +127,9 @@
     total = jnp.zeros((row_total,), jnp.float32)
     summed = jnp.zeros((row_total, value_width), jnp.float32)
     keys = lax.all_gather(comp_keys, "seq", axis=0, tiled=True)
-    values = lax.all_gather(comp_values, "seq", axis=0, tiled=True)
+    values = jnp.concatenate(
+        lax.all_to_all(jnp.stack(lax.axis_size("seq") * [comp_values]), "seq", 0, 0), axis=0
+    )
     length = keys.shape[0]
     block = length
     for size in (1024, 512, 256, 128):

time: 312 us -> 294 us (0.942)
  blocking collectives: 103 us -> 79.3 us
  waiting for transfers between devices: 39.3 us -> 49.1 us
  starting transfers between devices: 58.1 us -> 51 us
    all_gather x1 -> x0, blocking collectives: 88.1 us -> none  [shards(): values = lax.all_gather(comp_values, 'seq', axis=0, tiled=True)]
    all_gather x1, blocking collectives: 14.4 us -> 79.3 us  [shards(): keys = lax.all_gather(comp_keys, 'seq', axis=0, tiled=True)]
    all_to_all x1, waiting for transfers between devices: 0.01 us -> 46.3 us  [shards(): lax.all_to_all(value_block_list[safe], 'seq', split_axis=0, concat_axis=0...]
    ppermute x4, waiting for transfers between devices: 37.8 us -> 0.01 us  [from_behind(): return lax.ppermute(x, axis, pairs)]
    all_to_all x1, starting transfers between devices: 33.3 us -> 4.69 us  [shards(): lax.all_to_all(key_blocks[safe], 'seq', split_axis=0, concat_axis=0, tile...]
    all_to_all x1, starting transfers between devices: 5.08 us -> 22.5 us  [shards(): lax.all_to_all(value_block_list[safe], 'seq', split_axis=0, concat_axis=0...]
    all_to_all x0 -> x1, starting transfers between devices: none -> 4.18 us  [shards(): lax.all_to_all(jnp.stack(lax.axis_size('seq') * [comp_values]), 'seq', 0, 0)]
    unnamed x61 -> x59, local copies, waits for them, and re-layouts: 8.66 us -> 8.71 us
  transfers between devices with their start and end apart: 10 -> 11, of which waited for: 3 -> 2; matrix products, arithmetic and copies ran while one was open for 27% -> 29% of each run, Pallas kernels for 0% -> 0%
where the time goes in v1:
time: 294 us; the launch traced here: 292 us
  blocking collectives  79.3 us (27%)
  local copies, waits for them, and re-layouts  63 us (21%)
  starting transfers between devices  51 us (17%)
  waiting for transfers between devices  49.1 us (17%)
  matrix products  20.2 us (7%)
  other arithmetic  15.8 us (5%)
  between operations  14 us (5%)
    all_gather x1, blocking collectives, shards(): keys = lax.all_gather(comp_keys, 'seq', axis=0, tiled=True)  79.3 us
    all_to_all x1, waiting for transfers between devices, shards(): lax.all_to_all(value_block_list[safe], 'seq', split_axis=0, concat_axis=0...  46.3 us
    all_to_all x1, starting transfers between devices, shards(): lax.all_to_all(value_block_list[safe], 'seq', split_axis=0, concat_axis=0...  22.5 us
    ppermute x4, starting transfers between devices, from_behind(): return lax.ppermute(x, axis, pairs)  12.9 us
    scatter x1, local copies, waits for them, and re-layouts, shards(): jnp.full((ranks, capacity), -1, jnp.int32).at[owner, position].set(local)  10.2 us
    unnamed x59, local copies, waits for them, and re-layouts  8.71 us
    all_to_all x1, starting transfers between devices, shards(): lax.all_to_all(request, 'seq', split_axis=0, concat_axis=0, tiled=True)  6.14 us
    dot_general x2, matrix products, finish_rows(): jnp.matmul(weights.astype(jnp.bfloat16), values, preferred_element_type=j...  5.99 us
  transfers between devices with their start and end apart: 11, of which 2 were waited for; matrix products, arithmetic and copies ran while one was open for 29% of the time, Pallas kernels for 0%

profile of v1, /device:TPU:0, one launch (start us, length us, event | category | flops | bytes accessed | tf_op | source)
XLA Modules:
  0.0 292.5 jit_solution(4149696713774306006)
XLA Ops:
  6.5 0.7 all-gather.5.cloned.1.call-update
  7.3 0.9 slice.154
  8.7 0.9 slice_bitcast_fusion.1
  9.6 0.7 pad_maximum_fusion.2
  10.8 0.8 reshape.406
  12.3 1.3 reduce.7
  14.5 10.2 %scatter_fusion = s32[8,16]{1,0:T(8,128)} fusion(s32[8,16]{1,0:T(8,128)} %broadcast_in_dim.83, s32[64]{0:T(128)S(1)} %fusion.59, s32[64]{0:T(128)S(1)} %get-tuple-element.7), kind=kCustom, calls=%fused_computation.4 | custom fusion | bytes 1280 | tf_op jit(solution)/shard_map/scatter | solution.py:164
  24.7 6.1 %all-to-all-start.1 = ((s32[8,1,16]{2,1,0:T(1,128)}), s32[8,1,16]{2,1,0:T(1,128)}, u32[]{:S(2)}, u32[]{:S(2)}) async-start(s32[8,1,16]{2,1,0:T(1,128)} %bitcast.11), calls=%async_computation.1 | async-start | bytes 8192 | tf_op jit(solution)/shard_map/all_to_all | solution.py:168
  31.9 2.1 reshape.399
  34.0 2.1 reshape_reshape.6
  40.1 0.8 reshape.401
  41.1 0.7 reshape.412
  42.4 2.5 copy.51
  45.0 1.3 reshape.398
  46.3 1.4 copy.36
  47.7 0.7 copy.41
  48.4 0.7 copy.48
  49.9 1.0 broadcast_select_fusion
  50.9 1.6 pad_maximum_fusion
  52.5 4.6 %collective-permute-start.1 = (bf16[204800]{0:T(1024)(128)(2,1)}, bf16[204800]{0:T(1024)(128)(2,1)}, u32[]{:S(2)}, u32[]{:S(2)}) collective-permute-start(bf16[204800]{0:T(1024)(128)(2,1)} %pad_maximum_fusion), channel_id=1, source_target_pairs={{0,4},{1,5},{2,6},{3,7},{8,12},{9,13},{10,14},{11,15},{16,20},{17,... | collective-permute-start | bytes 1228808 | tf_op jit(solution)/shard_map/ppermute | solution.py:21
  57.1 3.6 %collective-permute-start.2 = (bf16[204800]{0:T(1024)(128)(2,1)}, bf16[204800]{0:T(1024)(128)(2,1)}, u32[]{:S(2)}, u32[]{:S(2)}) collective-permute-start(bf16[204800]{0:T(1024)(128)(2,1)} %pad_maximum_fusion), channel_id=1, source_target_pairs={{0,3},{1,4},{2,5},{3,6},{4,7},{8,11},{9,12},{10,13},{11,14},{12,15... | collective-permute-start | bytes 1228808 | tf_op jit(solution)/shard_map/ppermute | solution.py:21
  60.7 2.6 collective-permute-start.3
  63.3 2.1 collective-permute-start.4
  66.1 0.7 pad_maximum_fusion.3
  66.8 1.1 reshape.400
  67.9 1.3 fusion.45
  69.2 1.3 fusion.37
  71.2 4.2 %all-to-all-start = ((bf16[8,64,128]{2,1,0:T(8,128)(2,1)}), bf16[8,64,128]{2,1,0:T(8,128)(2,1)}, u32[]{:S(2)}, u32[]{:S(2)}) async-start(bf16[8,64,128]{2,1,0:T(8,128)(2,1)} %stack.2), calls=%async_computation | async-start | bytes 262144 | tf_op jit(solution)/shard_map/all_to_all | solution.py:131
  75.4 2.8 gather_fusion
  78.2 2.2 gather_fusion.2
  81.2 0.9 pad_maximum_fusion.1
  82.2 1.2 copy.39
  83.4 1.3 reshape.397
  84.7 1.4 all-to-all-done
  86.1 22.5 %all-to-all-start.3 = ((bf16[8,16,64,128]{3,2,1,0:T(8,128)(2,1)}), bf16[8,16,64,128]{3,2,1,0:T(8,128)(2,1)}, u32[]{:S(2)}, u32[]{:S(2)}) async-start(bf16[8,16,64,128]{3,2,1,0:T(8,128)(2,1)} %bitcast.114), calls=%async_computation.3 | async-start | bytes 4194304 | tf_op jit(solution)/shard_map/all_to_all | solution.py:171
  108.7 1.5 fusion.49
  110.2 1.4 fusion.54
  111.5 46.3 %all-to-all-done.3 = bf16[8,16,64,128]{3,2,1,0:T(8,128)(2,1)} async-done(((bf16[8,16,64,128]{3,2,1,0:T(8,128)(2,1)}), bf16[8,16,64,128]{3,2,1,0:T(8,128)(2,1)}, u32[]{:S(2)}, u32[]{:S(2)}) %all-to-all-start.3) | async-done | bytes 2097184 | tf_op jit(solution)/shard_map/all_to_all | solution.py:171
  157.8 4.7 %all-to-all-start.2 = ((bf16[8,16,64,192]{3,2,1,0:T(8,128)(2,1)}), bf16[8,16,64,192]{3,2,1,0:T(8,128)(2,1)}, u32[]{:S(2)}, u32[]{:S(2)}) async-start(bf16[8,16,64,192]{3,2,1,0:T(8,128)(2,1)} %bitcast.111), calls=%async_computation.2 | async-start | bytes 8388608 | tf_op jit(solution)/shard_map/all_to_all | solution.py:170
  162.5 1.4 fusion.53
  164.1 0.8 slice.206
  165.0 0.8 slice.207
  165.9 0.8 slice.208
  166.8 0.8 slice.209
  167.7 1.4 fusion.52
  169.1 1.4 fusion.51
  171.9 3.2 %fusion.65 = (f32[2048]{0:T(1024)S(1)}, f32[2048,1152]{0,1:T(8,128)S(1)}) fusion(pred[2048,1152]{0,1:T(32,128)(4,1)S(1)} %copy.51, bf16[1152,192]{1,0:T(8,128)(2,1)S(1)} %constant_dynamic-update-slice_fusion.1, bf16[2048,192]{1,0:T(8,128)(2,1)} %reshape.399), kind=kOutput, calls=%fused_computation.126 | convolution fusion | flops 913045504 | bytes 13033472 | tf_op jit(solution)/shard_map/rd,kd->rk/dot_general | solution.py:196
  175.1 1.4 fusion.1
  176.4 2.8 fusion.16
  179.3 1.2 reshape.419
  180.4 1.8 fusion.23
  182.2 1.8 fusion.30
  184.0 79.3 %all_gather.10 = bf16[512,192]{1,0:T(8,128)(2,1)S(1)} all-gather(bf16[64,192]{1,0:T(8,128)(2,1)S(1)} %fusion.30), channel_id=1, replica_groups=mesh['kv'=4,'seq'=8] {'seq'}, dimensions={0}, use_global_device_ids=true | all-gather | bytes 221184 | tf_op jit(solution)/shard_map/all_gather | solution.py:129
  263.3 0.9 fusion.12
  264.2 0.9 fusion.13
  265.1 2.4 fusion.15
  267.6 1.1 reshape.403
  268.7 3.5 %gather_fusion.3 = bf16[64,64,128]{2,1,0:T(8,128)(2,1)} fusion(bf16[128,64,128]{2,1,0:T(8,128)(2,1)} %bitcast.21, s32[1024]{0:T(1024)} %pad_clamp_fusion), kind=kCustom, calls=%fused_computation.3 | custom fusion | bytes 2097408 | tf_op jit(solution)/shard_map/gather | solution.py:177
  272.2 3.0 %gather_fusion.1 = bf16[64,64,192]{2,1,0:T(8,128)(2,1)S(1)} fusion(bf16[128,64,192]{2,1,0:T(8,128)(2,1)} %bitcast.15, s32[1024]{0:T(1024)} %pad_clamp_fusion), kind=kCustom, calls=%fused_computation.1 | custom fusion | bytes 3145984 | tf_op jit(solution)/shard_map/gather | solution.py:176
  275.2 1.3 bitcast_reduce_fusion
  276.5 1.4 fusion.3
  277.9 3.2 %fusion.41 = f32[4,512,128]{2,1,0:T(8,128)} fusion(bf16[4,1024,128]{2,1,0:T(8,128)(2,1)S(1)} %bitcast.120, f32[4,1024,512]{2,1,0:T(8,128)S(1)} %get-tuple-element.17, f32[4,512]{1,0:T(4,128)S(1)} %get-tuple-element.16, f32[4,512]{1,0:T(4,128)S(1)} %fusion.3), kind=kOutput, calls=%fused_computation.50 | convolution fusion | flops 543424512 | bytes 10502144 | tf_op jit(solution)/shard_map/dot_general | solution.py:38
  281.1 1.5 reshape_reshape.7
  283.7 1.9 fusion.39
  (122 shorter events, 14.2 us)
Async XLA Ops:
  6.5 25.1 %copy-start.7 = (bf16[1024,192]{0,1:T(8,128)(2,1)S(1)}, bf16[1024,192]{0,1:T(8,128)(2,1)}, u32[]{:S(2)}) copy-start(bf16[1024,192]{0,1:T(8,128)(2,1)} %param.10) | copy-start | bytes 1179652
  6.5 25.3 %copy-start.2 = (bf16[128,3072]{1,0:T(8,128)(2,1)S(1)}, bf16[128,3072]{1,0:T(8,128)(2,1)}, u32[]{:S(2)}) copy-start(bf16[128,3072]{1,0:T(8,128)(2,1)} %param.9) | copy-start | bytes 2359300
  6.5 61.4 %all-gather.5.cloned.1.call-start = ((), (), s32[]{:S(2)}) async-start(), calls=%async_computation.5 | async-start | bytes 1310720 | tf_op jit(solution)/shard_map/all_gather | solution.py:66
  10.3 28.1 %copy-start.18 = (bf16[16,192,3]{1,0,2:T(8,128)(2,1)S(1)}, bf16[16,192,3]{1,0,2:T(8,128)(2,1)}, u32[]{:S(2)}) copy-start(bf16[16,192,3]{1,0,2:T(8,128)(2,1)} %param.17) | copy-start | bytes 55300
  10.3 39.6 %collective-permute-start = (bf16[163840]{0:T(1024)(128)(2,1)}, bf16[163840]{0:T(1024)(128)(2,1)}, u32[]{:S(2)}, u32[]{:S(2)}) collective-permute-start(bf16[163840]{0:T(1024)(128)(2,1)} %pad_maximum_fusion.2), channel_id=1, source_target_pairs={{7,0},{0,1},{1,2},{2,3},{3,4},{4,5},{5,6},{6,7},{15,8},{8,9},{9,10... | collective-permute-start | bytes 983048 | tf_op jit(solution)/shard_map/ppermute | solution.py:15
  24.7 24.5 %all-to-all-start.1 = ((s32[8,1,16]{2,1,0:T(1,128)}), s32[8,1,16]{2,1,0:T(1,128)}, u32[]{:S(2)}, u32[]{:S(2)}) async-start(s32[8,1,16]{2,1,0:T(1,128)} %bitcast.11), calls=%async_computation.1 | async-start | bytes 8192 | tf_op jit(solution)/shard_map/all_to_all | solution.py:168
  30.8 9.3 %copy-start = (bf16[1024,128]{1,0:T(8,128)(2,1)S(1)}, bf16[1024,128]{1,0:T(8,128)(2,1)}, u32[]{:S(2)}) copy-start(bf16[1024,128]{1,0:T(8,128)(2,1)} %param.11) | copy-start | bytes 786436
  30.8 149.6 %all-gather.3.cloned.1.call-start = ((), (), s32[]{:S(2)}) async-start(), calls=%async_computation.4 | async-start | bytes 2949120 | tf_op jit(solution)/shard_map/all_gather | solution.py:65
  31.6 9.4 %copy-start.17 = (bf16[128,192]{0,1:T(8,128)(2,1)S(1)}, bf16[128,192]{0,1:T(8,128)(2,1)}, u32[]{:S(2)}) copy-start(bf16[128,192]{0,1:T(8,128)(2,1)} %param.12) | copy-start | bytes 147460
  41.1 0.8 copy-start.9
  42.4 23.7 %slice-start = ((bf16[1024,128]{1,0:T(8,128)(2,1)}), bf16[1008,128]{1,0:T(8,128)(2,1)S(1)}, s32[]{:S(2)}) async-start(bf16[1024,128]{1,0:T(8,128)(2,1)} %param.11), calls=%async_computation.6 | async-start | bytes 516096 | tf_op jit(solution)/shard_map/slice | solution.py:106
  52.5 56.1 %collective-permute-start.1 = (bf16[204800]{0:T(1024)(128)(2,1)}, bf16[204800]{0:T(1024)(128)(2,1)}, u32[]{:S(2)}, u32[]{:S(2)}) collective-permute-start(bf16[204800]{0:T(1024)(128)(2,1)} %pad_maximum_fusion), channel_id=1, source_target_pairs={{0,4},{1,5},{2,6},{3,7},{8,12},{9,13},{10,14},{11,15},{16,20},{17,... | collective-permute-start | bytes 1228808 | tf_op jit(solution)/shard_map/ppermute | solution.py:21
  57.1 51.5 %collective-permute-start.2 = (bf16[204800]{0:T(1024)(128)(2,1)}, bf16[204800]{0:T(1024)(128)(2,1)}, u32[]{:S(2)}, u32[]{:S(2)}) collective-permute-start(bf16[204800]{0:T(1024)(128)(2,1)} %pad_maximum_fusion), channel_id=1, source_target_pairs={{0,3},{1,4},{2,5},{3,6},{4,7},{8,11},{9,12},{10,13},{11,14},{12,15... | collective-permute-start | bytes 1228808 | tf_op jit(solution)/shard_map/ppermute | solution.py:21
  60.7 48.0 %collective-permute-start.3 = (bf16[204800]{0:T(1024)(128)(2,1)}, bf16[204800]{0:T(1024)(128)(2,1)}, u32[]{:S(2)}, u32[]{:S(2)}) collective-permute-start(bf16[204800]{0:T(1024)(128)(2,1)} %pad_maximum_fusion), channel_id=1, source_target_pairs={{0,2},{1,3},{2,4},{3,5},{4,6},{5,7},{8,10},{9,11},{10,12},{11,13},... | collective-permute-start | bytes 1228808 | tf_op jit(solution)/shard_map/ppermute | solution.py:21
  63.3 45.4 %collective-permute-start.4 = (bf16[204800]{0:T(1024)(128)(2,1)}, bf16[204800]{0:T(1024)(128)(2,1)}, u32[]{:S(2)}, u32[]{:S(2)}) collective-permute-start(bf16[204800]{0:T(1024)(128)(2,1)} %pad_maximum_fusion), channel_id=1, source_target_pairs={{0,1},{1,2},{2,3},{3,4},{4,5},{5,6},{6,7},{8,9},{9,10},{10,11},{11... | collective-permute-start | bytes 1228808 | tf_op jit(solution)/shard_map/ppermute | solution.py:21
  71.2 14.9 %all-to-all-start = ((bf16[8,64,128]{2,1,0:T(8,128)(2,1)}), bf16[8,64,128]{2,1,0:T(8,128)(2,1)}, u32[]{:S(2)}, u32[]{:S(2)}) async-start(bf16[8,64,128]{2,1,0:T(8,128)(2,1)} %stack.2), calls=%async_computation | async-start | bytes 262144 | tf_op jit(solution)/shard_map/all_to_all | solution.py:131
  75.4 2.8 copy-start.1
  86.1 71.7 %all-to-all-start.3 = ((bf16[8,16,64,128]{3,2,1,0:T(8,128)(2,1)}), bf16[8,16,64,128]{3,2,1,0:T(8,128)(2,1)}, u32[]{:S(2)}, u32[]{:S(2)}) async-start(bf16[8,16,64,128]{3,2,1,0:T(8,128)(2,1)} %bitcast.114), calls=%async_computation.3 | async-start | bytes 4194304 | tf_op jit(solution)/shard_map/all_to_all | solution.py:171
  157.8 13.3 %copy-start.16 = (bf16[128,128]{1,0:T(8,128)(2,1)S(1)}, bf16[128,128]{1,0:T(8,128)(2,1)}, u32[]{:S(2)}) copy-start(bf16[128,128]{1,0:T(8,128)(2,1)} %param.13) | copy-start | bytes 98308
  157.8 14.0 %copy-start.10 = (bf16[128,192]{1,0:T(8,128)(2,1)S(1)}, bf16[128,192]{1,0:T(8,128)(2,1)}, u32[]{:S(2)}) copy-start(bf16[128,192]{1,0:T(8,128)(2,1)} %copy-done.9) | copy-start | bytes 147460
  157.8 114.4 %all-to-all-start.2 = ((bf16[8,16,64,192]{3,2,1,0:T(8,128)(2,1)}), bf16[8,16,64,192]{3,2,1,0:T(8,128)(2,1)}, u32[]{:S(2)}, u32[]{:S(2)}) async-start(bf16[8,16,64,192]{3,2,1,0:T(8,128)(2,1)} %bitcast.111), calls=%async_computation.2 | async-start | bytes 8388608 | tf_op jit(solution)/shard_map/all_to_all | solution.py:170
  176.4 4.0 %copy-start.11 = (bf16[64,3072]{1,0:T(8,128)(2,1)S(1)}, bf16[64,3072]{1,0:T(8,128)(2,1)}, u32[]{:S(2)}) copy-start(bf16[64,3072]{1,0:T(8,128)(2,1)} %reshape.398) | copy-start | bytes 1179652
  176.4 5.8 %copy-start.12 = (bf16[64,3072]{1,0:T(8,128)(2,1)S(1)}, bf16[64,3072]{1,0:T(8,128)(2,1)}, u32[]{:S(2)}) copy-start(bf16[64,3072]{1,0:T(8,128)(2,1)} %reshape.397) | copy-start | bytes 1179652
  179.3 84.1 %copy-start.4 = (bf16[2048,192]{1,0:T(8,128)(2,1)S(1)}, bf16[2048,192]{1,0:T(8,128)(2,1)}, u32[]{:S(2)}) copy-start(bf16[2048,192]{1,0:T(8,128)(2,1)} %reshape.399) | copy-start | bytes 2359300
  179.3 84.1 %copy-start.19 = (pred[512]{0:T(512)(128)(4,1)S(1)}, pred[512]{0:T(512)(128)(4,1)}, u32[]{:S(2)}) copy-start(pred[512]{0:T(512)(128)(4,1)} %iota_compare_fusion.1) | copy-start | bytes 1540
  267.6 7.6 %copy-start.3 = (bf16[4,512,192]{2,1,0:T(8,128)(2,1)S(1)}, bf16[4,512,192]{2,1,0:T(8,128)(2,1)}, u32[]{:S(2)}) copy-start(bf16[4,512,192]{2,1,0:T(8,128)(2,1)} %reshape_reshape.6) | copy-start | bytes 2359300
  276.5 1.4 copy-start.8
  277.9 4.7 %copy-start.13 = (f32[128,16]{1,0:T(8,128)S(1)}, f32[128,16]{1,0:T(8,128)}, u32[]{:S(2)}) copy-start(f32[128,16]{1,0:T(8,128)} %copy.36) | copy-start | bytes 24580
  277.9 5.1 %copy-start.14 = (f32[128,16]{1,0:T(8,128)S(1)}, f32[128,16]{1,0:T(8,128)}, u32[]{:S(2)}) copy-start(f32[128,16]{1,0:T(8,128)} %copy.41) | copy-start | bytes 24580
  281.1 2.2 copy-start.15
  281.1 2.6 copy-start.5
  281.1 2.6 copy-start.6
Sparse Core Ops, SparseCore 0:
  9.2 29.2 all-gather.4
  40.3 37.3 all-gather.2
